TPU v7x, 32 devices: a whole 2x2x4 slice. The times are simulated.
32 devices in a mesh: dp: 16 (over z, y, x), head: 2 (over core).
Axes of the slice: x: 2, y: 2, z: 4, core: 2. Of those that a mesh axis runs over, the one named last changes fastest.
Arguments:
- tokens: bfloat16 [8192, 2048], P('dp'), may hold values from -6 to 6
- seq_count: int32 [16], P('dp'), may hold values from 1 to 2
- valid_len: int32 [32], P('dp'), may hold values from 128 to 256
- attn_gain: bfloat16 [2048], P('dp'), may hold values from 0.5 to 1.5
- ffn_gain: bfloat16 [2048], P('dp'), may hold values from 0.5 to 1.5
- q_weight: bfloat16 [2048, 2048], P('dp', 'head'), may hold values from -0.25 to 0.25
- k_weight: bfloat16 [2048, 2048], P('dp', 'head'), may hold values from -0.25 to 0.25
- v_weight: bfloat16 [2048, 2048], P('dp', 'head'), may hold values from -0.125 to 0.125
- forget_weight: bfloat16 [2048, 256], P('dp', 'head'), may hold values from -0.125 to 0.125
- out_weight: bfloat16 [2048, 2048], P('dp', 'head'), may hold values from -1.5 to 1.5
- gate_weight: bfloat16 [2048, 5632], P('dp', 'head'), may hold values from -0.125 to 0.125
- up_weight: bfloat16 [2048, 5632], P('dp', 'head'), may hold values from -0.125 to 0.125
- down_weight: bfloat16 [2048, 5632], P('dp', 'head'), may hold values from -0.078125 to 0.078125
- cotangent: float32 [8192, 2048], P('dp'), may hold values from -6 to 6
Outputs:
- block_out: bfloat16 [8192, 2048], P('dp')
- input_grad: float32 [8192, 2048], P('dp')
- attn_gain_grad: float32 [2048], P('dp')
- ffn_gain_grad: float32 [2048], P('dp')
- q_grad: float32 [2048, 2048], P('dp', 'head')
- k_grad: float32 [2048, 2048], P('dp', 'head')
- v_grad: float32 [2048, 2048], P('dp', 'head')
- forget_grad: float32 [2048, 256], P('dp', 'head')
- out_grad: float32 [2048, 2048], P('dp', 'head')
- gate_grad: float32 [2048, 5632], P('dp', 'head')
- up_grad: float32 [2048, 5632], P('dp', 'head')
- down_grad: float32 [2048, 5632], P('dp', 'head')
All inputs are finite; a program needn't handle non-finite values.
Results may differ from a plain program's by a relative error of at most 0.0089.
Values may be sent and summed in bfloat16 or wider, within the bound.
A program may use at most 256 MiB of HBM per device.

v0:
```python
import jax
import jax.numpy as jnp
from jax import lax
from jax.sharding import PartitionSpec as P

SLOTS = 64
KDIM = 512
SEQ_LEN = 256


def einsum_high(form, left, right):
    return jnp.einsum(form, left, right, precision=lax.Precision.HIGHEST)


def times_trans(left, right):
    return lax.dot_general(
        left, right, (((1,), (1,)), ((), ())), preferred_element_type=jnp.float32
    )


def outer_sum(left, right):
    return lax.dot_general(
        left, right, (((0,), (0,)), ((), ())), preferred_element_type=jnp.float32
    )


def rms_norm(values, gain):
    return values * lax.rsqrt(jnp.mean(values * values, axis=-1, keepdims=True) + 1e-06) * gain


def swiglu(gate_vals, up_vals):
    return jax.nn.silu(gate_vals) * up_vals


def block_step(states, block):
    key_state, value_state = states
    query_block, key_block, value_block, forget_block = block
    width = query_block.shape[0]
    totals = jnp.cumsum(forget_block, axis=0)
    writes = -jnp.expm1(forget_block)
    order = jnp.arange(width, dtype=jnp.int32)
    lower = (order[:, None] >= order[None, :])[:, :, None]
    spread = jnp.where(lower, totals[:, None, :] - totals[None, :, :], 0.0)
    decays = jnp.where(lower, jnp.exp(spread), 0.0) * writes[None, :, :]
    products = einsum_high("td,id->ti", query_block, key_block)
    carried = jnp.exp(totals)
    scores = einsum_high("ti,tim->tm", products, decays) + carried * einsum_high(
        "td,md->tm", query_block, key_state
    )
    weights = jax.nn.softmax(scores, axis=-1)
    mixing = einsum_high("tm,tim->ti", weights, decays)
    result = einsum_high("ti,id->td", mixing, value_block) + einsum_high(
        "tm,md->td", weights * carried, value_state
    )
    final = totals[-1]
    tails = jnp.exp(final[None, :] - totals) * writes
    key_next = jnp.exp(final)[:, None] * key_state + einsum_high("im,id->md", tails, key_block)
    value_next = jnp.exp(final)[:, None] * value_state + einsum_high(
        "im,id->md", tails, value_block
    )
    return ((key_next, value_next), result)


def scan_slots(query, keys, values_in, forget):
    width = min(64, SEQ_LEN)
    count = SEQ_LEN // width
    pieces = (
        query.reshape(count, width, KDIM),
        keys.reshape(count, width, KDIM),
        values_in.reshape(count, width, KDIM),
        forget.reshape(count, width, SLOTS),
    )
    start = (jnp.zeros((SLOTS, KDIM), jnp.float32), jnp.zeros((SLOTS, KDIM), jnp.float32))
    ignored, outputs = lax.scan(jax.checkpoint(block_step), start, pieces)
    return outputs.reshape(SEQ_LEN, KDIM)


def mixer(query_proj, key_proj, value_proj, forget_proj):
    rows = query_proj.shape[0]
    seq_total = rows // SEQ_LEN
    head_total = forget_proj.shape[1] // SLOTS

    def split(values, width):
        shaped = values.reshape(seq_total, SEQ_LEN, head_total, width).transpose(0, 2, 1, 3)
        return shaped.reshape(seq_total * head_total, SEQ_LEN, width)

    query = split(jax.nn.silu(query_proj), KDIM) * KDIM ** (-0.5)
    keys = split(jax.nn.silu(key_proj), KDIM)
    values_in = split(value_proj, KDIM)
    forget = split(jax.nn.log_sigmoid(forget_proj) / 8.0, SLOTS)
    outputs = jax.vmap(scan_slots)(query, keys, values_in, forget)
    outputs = outputs.reshape(seq_total, head_total, SEQ_LEN, KDIM).transpose(0, 2, 1, 3)
    return outputs.reshape(rows, head_total * KDIM)


def body(
    tokens,
    seq_count,
    valid_len,
    attn_gain,
    ffn_gain,
    q_weight,
    k_weight,
    v_weight,
    forget_weight,
    out_weight,
    gate_weight,
    up_weight,
    down_weight,
    cotangent,
):
    shards = (
        attn_gain,
        ffn_gain,
        q_weight,
        k_weight,
        v_weight,
        forget_weight,
        out_weight,
        gate_weight,
        up_weight,
        down_weight,
    )
    whole = (
        lax.all_gather(shards[0], "dp", axis=0, tiled=True),
        lax.all_gather(shards[1], "dp", axis=0, tiled=True),
        lax.all_gather(shards[2], "dp", axis=0, tiled=True),
        lax.all_gather(shards[3], "dp", axis=0, tiled=True),
        lax.all_gather(shards[4], "dp", axis=0, tiled=True),
        lax.all_gather(shards[5], "dp", axis=0, tiled=True),
        lax.all_gather(shards[6], "dp", axis=0, tiled=True),
        lax.all_gather(shards[7], "dp", axis=0, tiled=True),
        lax.all_gather(shards[8], "dp", axis=0, tiled=True),
        lax.all_gather(shards[9], "dp", axis=0, tiled=True),
    )
    gain_attn, gain_ffn, w_query, w_key, w_value, w_forget, w_out, w_gate, w_up, w_down = whole
    rows = tokens.shape[0]
    places = jnp.arange(rows, dtype=jnp.int32)
    slot_ids = places // SEQ_LEN
    inside = places % SEQ_LEN
    slot_range = jnp.arange(valid_len.shape[0], dtype=jnp.int32)
    lengths = jnp.sum(
        jnp.where(slot_ids[:, None] == slot_range[None, :], valid_len[None, :], 0), axis=1
    )
    live = ((slot_ids < seq_count[0]) & (inside < lengths)).astype(jnp.float32)[:, None]
    inputs = tokens.astype(jnp.float32)
    normed_attn, attn_norm_back = jax.vjp(rms_norm, inputs, gain_attn.astype(jnp.float32))
    attn_in = normed_attn.astype(jnp.bfloat16)
    query_proj = jnp.dot(attn_in, w_query, preferred_element_type=jnp.float32)
    key_proj = jnp.dot(attn_in, w_key, preferred_element_type=jnp.float32)
    value_proj = jnp.dot(attn_in, w_value, preferred_element_type=jnp.float32)
    forget_proj = jnp.dot(attn_in, w_forget, preferred_element_type=jnp.float32)
    mixed_full, mixer_back = jax.vjp(mixer, query_proj, key_proj, value_proj, forget_proj)
    mixed = mixed_full.astype(jnp.bfloat16)
    attn = lax.psum(times_trans(mixed, w_out), "head")
    resid = inputs + attn
    normed_ffn, ffn_norm_back = jax.vjp(rms_norm, resid, gain_ffn.astype(jnp.float32))
    ffn_in = normed_ffn.astype(jnp.bfloat16)
    gate_vals = jnp.dot(ffn_in, w_gate, preferred_element_type=jnp.float32)
    up_vals = jnp.dot(ffn_in, w_up, preferred_element_type=jnp.float32)
    hidden_full, glu_back = jax.vjp(swiglu, gate_vals, up_vals)
    hidden = hidden_full.astype(jnp.bfloat16)
    ffn = lax.psum(times_trans(hidden, w_down), "head")
    block_out = (live * (resid + ffn)).astype(jnp.bfloat16)
    again = (
        lax.all_gather(shards[0], "dp", axis=0, tiled=True),
        lax.all_gather(shards[1], "dp", axis=0, tiled=True),
        lax.all_gather(shards[2], "dp", axis=0, tiled=True),
        lax.all_gather(shards[3], "dp", axis=0, tiled=True),
        lax.all_gather(shards[4], "dp", axis=0, tiled=True),
        lax.all_gather(shards[5], "dp", axis=0, tiled=True),
        lax.all_gather(shards[6], "dp", axis=0, tiled=True),
        lax.all_gather(shards[7], "dp", axis=0, tiled=True),
        lax.all_gather(shards[8], "dp", axis=0, tiled=True),
        lax.all_gather(shards[9], "dp", axis=0, tiled=True),
    )
    gain_attn, gain_ffn, w_query, w_key, w_value, w_forget, w_out, w_gate, w_up, w_down = again
    grad_res = live * cotangent
    grad_ffn = grad_res.astype(jnp.bfloat16)
    grad_down = outer_sum(grad_ffn, hidden)
    grad_hidden = jnp.dot(grad_ffn, w_down, preferred_element_type=jnp.float32)
    grad_gate_vals, grad_up_vals = glu_back(grad_hidden)
    gate_low = grad_gate_vals.astype(jnp.bfloat16)
    up_low = grad_up_vals.astype(jnp.bfloat16)
    grad_gate = outer_sum(ffn_in, gate_low)
    grad_up = outer_sum(ffn_in, up_low)
    grad_ffn_in = lax.psum(times_trans(gate_low, w_gate) + times_trans(up_low, w_up), "head")
    grad_resid_norm, grad_gain_ffn = ffn_norm_back(grad_ffn_in)
    grad_resid = grad_res + grad_resid_norm
    grad_attn = grad_resid.astype(jnp.bfloat16)
    grad_out = outer_sum(grad_attn, mixed)
    grad_mixed = jnp.dot(grad_attn, w_out, preferred_element_type=jnp.float32)
    grad_qproj, grad_kproj, grad_vproj, grad_fproj = mixer_back(grad_mixed)
    query_low = grad_qproj.astype(jnp.bfloat16)
    key_low = grad_kproj.astype(jnp.bfloat16)
    value_low = grad_vproj.astype(jnp.bfloat16)
    forget_low = grad_fproj.astype(jnp.bfloat16)
    grad_query = outer_sum(attn_in, query_low)
    grad_key = outer_sum(attn_in, key_low)
    grad_value = outer_sum(attn_in, value_low)
    grad_forget = outer_sum(attn_in, forget_low)
    local_in = (
        times_trans(query_low, w_query)
        + times_trans(key_low, w_key)
        + times_trans(value_low, w_value)
        + times_trans(forget_low, w_forget)
    )
    grad_attn_in = lax.psum(local_in, "head")
    grad_input_norm, grad_gain_attn = attn_norm_back(grad_attn_in)
    input_grad = grad_resid + grad_input_norm
    reduced = (
        lax.psum_scatter(grad_gain_attn, "dp", scatter_dimension=0, tiled=True),
        lax.psum_scatter(grad_gain_ffn, "dp", scatter_dimension=0, tiled=True),
        lax.psum_scatter(grad_query, "dp", scatter_dimension=0, tiled=True),
        lax.psum_scatter(grad_key, "dp", scatter_dimension=0, tiled=True),
        lax.psum_scatter(grad_value, "dp", scatter_dimension=0, tiled=True),
        lax.psum_scatter(grad_forget, "dp", scatter_dimension=0, tiled=True),
        lax.psum_scatter(grad_out, "dp", scatter_dimension=0, tiled=True),
        lax.psum_scatter(grad_gate, "dp", scatter_dimension=0, tiled=True),
        lax.psum_scatter(grad_up, "dp", scatter_dimension=0, tiled=True),
        lax.psum_scatter(grad_down, "dp", scatter_dimension=0, tiled=True),
    )
    return (
        block_out,
        input_grad,
        reduced[0],
        reduced[1],
        reduced[2],
        reduced[3],
        reduced[4],
        reduced[5],
        reduced[6],
        reduced[7],
        reduced[8],
        reduced[9],
    )


def solution(mesh):
    in_specs = (
        P("dp", None),
        P("dp"),
        P("dp"),
        P("dp"),
        P("dp"),
        P("dp", "head"),
        P("dp", "head"),
        P("dp", "head"),
        P("dp", "head"),
        P("dp", "head"),
        P("dp", "head"),
        P("dp", "head"),
        P("dp", "head"),
        P("dp", None),
    )
    out_specs = (
        P("dp", None),
        P("dp", None),
        P("dp"),
        P("dp"),
        P("dp", "head"),
        P("dp", "head"),
        P("dp", "head"),
        P("dp", "head"),
        P("dp", "head"),
        P("dp", "head"),
        P("dp", "head"),
        P("dp", "head"),
    )
    return jax.shard_map(body, mesh=mesh, in_specs=in_specs, out_specs=out_specs, check_vma=False)
```

profile of v0, /device:TPU:10, one launch (start us, length us, event | category | flops | bytes accessed | tf_op | source)
XLA Modules:
  0.0 3717.7 jit_solution(2996730783707626634)
XLA Ops:
  14.0 35.8 all_gather.39
  49.8 40.5 %all-gather = bf16[16,1,128]{2,1,0:T(2,128)(2,1)S(1)} all-gather(bf16[1,1,128]{2,1,0:T(2,128)(2,1)S(1)} %bitcast.437), channel_id=1, replica_groups=mesh['dp'=16,'head'=2] {'dp'}, dimensions={0}, use_global_device_ids=true | all-gather | bytes 4352 | tf_op jit(solution)/shard_map/all_gather | solution.py:125
  96.4 6.8 fusion.132
  110.8 57.6 %all-gather.12.cloned.1.call-done = bf16[2048,1024]{1,0:T(8,128)(2,1)} async-done(((bf16[128,1024]{1,0:T(8,128)(2,1)}), bf16[2048,1024]{1,0:T(8,128)(2,1)}) %all-gather.12.cloned.1.call-update) | async-done | bytes 4194320 | tf_op jit(solution)/shard_map/all_gather | solution.py:129
  168.4 5.9 fusion.165
  181.9 64.0 %all-gather.14.cloned.1.call-done = bf16[2048,1024]{1,0:T(8,128)(2,1)} async-done(((bf16[128,1024]{1,0:T(8,128)(2,1)}), bf16[2048,1024]{1,0:T(8,128)(2,1)}) %all-gather.14.cloned.1.call-update) | async-done | bytes 4194320 | tf_op jit(solution)/shard_map/all_gather | solution.py:127
  245.9 6.8 multiply_multiply_fusion.1
  260.2 175.8 %while.48 = (s32[]{:T(128)}, f32[4,64,512]{2,1,0:T(8,128)S(1)}, f32[4,64,512]{2,1,0:T(8,128)S(1)}, bf16[4,4,64,512]{3,2,0,1:T(8,128)(2,1)}, f32[4,4,64,512]{3,2,...) while((s32[]{:T(128)}, f32[4,64,512]{2,1,0:T(8,128)S(1)}, ...), condition=%wide.region_6.7_spmd.clone.clone, body=%wide.region_2.6_spmd.clone.clone.sunk | while | flops 640237632 | bytes 21779780 | solution.py:74
  265.7 10.1 fusion.402
  284.2 15.7 fusion.406
  309.5 10.1 fusion.402
  328.0 15.7 fusion.406
  353.3 10.1 fusion.402
  371.8 15.7 fusion.406
  397.1 10.1 fusion.402
  415.6 15.7 fusion.406
  438.6 6.9 fusion.180
  447.7 29.5 all-gather.1
  483.3 133.9 %all-gather.18.cloned.1.call-done = bf16[2048,2816]{1,0:T(8,128)(2,1)} async-done(((bf16[128,2816]{1,0:T(8,128)(2,1)}), bf16[2048,2816]{1,0:T(8,128)(2,1)}) %all-gather.18.cloned.1.call-update) | async-done | bytes 11534352 | tf_op jit(solution)/shard_map/all_gather | solution.py:132
  617.2 11.3 fusion.181
  628.5 132.2 %all-gather.20.cloned.1.call-done = bf16[2048,2816]{1,0:T(8,128)(2,1)} async-done(((bf16[128,2816]{1,0:T(8,128)(2,1)}), bf16[2048,2816]{1,0:T(8,128)(2,1)}) %all-gather.20.cloned.1.call-update) | async-done | bytes 11534352 | tf_op jit(solution)/shard_map/all_gather | solution.py:133
  760.7 11.1 fusion.182
  771.8 132.4 %all-gather.22.cloned.1.call-done = bf16[2048,2816]{1,0:T(8,128)(2,1)} async-done(((bf16[128,2816]{1,0:T(8,128)(2,1)}), bf16[2048,2816]{1,0:T(8,128)(2,1)}) %all-gather.22.cloned.1.call-update) | async-done | bytes 11534352 | tf_op jit(solution)/shard_map/all_gather | solution.py:134
  904.2 16.3 multiply_convert_fusion
  920.5 12.4 fusion.184
  932.9 9.2 convolution_add_fusion.8
  942.3 11.4 fusion.183
  953.7 17.6 all-reduce.11.cloned.1.call-done
  995.3 389.0 %while.47 = (s32[]{:T(128)}, f32[4,64,512]{2,1,0:T(8,128)S(1)}, f32[4,64,512]{2,1,0:T(8,128)}, f32[4,4,64,512]{3,2,0,1:T(8,128)}, f32[4,4,64,512]{3,2,0,1:T(8,12...) while((s32[]{:T(128)}, f32[4,64,512]{2,1,0:T(8,128)S(1)}, ...), condition=%wide.region_24.25_spmd.clone, body=%wide.region_12.24_spmd.clone.sunk | while | flops 1495470592 | bytes 52910904 | solution.py:74
  1007.9 9.1 fusion.373
  1024.4 10.1 fusion.377
  1043.2 15.4 fusion.380
  1063.1 14.9 fusion.385
  1078.7 6.4 fusion.387
  1103.0 9.1 fusion.373
  1119.8 10.1 fusion.377
  1138.6 15.4 fusion.380
  1158.2 15.1 fusion.385
  1174.1 6.4 fusion.387
  1198.4 9.1 fusion.373
  1215.0 10.1 fusion.377
  1233.9 15.4 fusion.380
  1253.6 14.9 fusion.385
  1269.3 6.4 fusion.387
  1293.8 9.1 fusion.373
  1310.3 10.1 fusion.377
  1329.1 15.4 fusion.380
  1349.0 14.9 fusion.385
  1364.6 6.4 fusion.387
  1414.1 7.8 fusion.161
  1422.0 6.2 fusion.159
  1436.6 9.0 fusion.133
  1445.7 13.6 fusion.188
  1459.4 13.1 fusion.189
  1473.1 13.4 fusion.153
  1492.0 71.4 %all-reduce.3 = (f32[2048]{0:T(1024)S(1)}, f32[2048]{0:T(1024)S(1)}) all-reduce(f32[2048]{0:T(1024)S(1)} %get-tuple-element.678, f32[2048]{0:T(1024)S(1)} %copy-done.49), channel_id=2, replica_groups=mesh['dp'=16,'head'=2] {'dp'}, use_global_device_ids=true, to_apply=%region_28.29.clone | all-reduce | flops 4096 | bytes 32768
  1564.6 9.5 fusion.123
  1574.0 139.0 %reduce-scatter.9.cloned.1.call-done = f32[128,1024]{1,0:T(8,128)} async-done(((f32[2048,1024]{1,0:T(8,128)}), f32[128,1024]{1,0:T(8,128)}) %reduce-scatter.9.cloned.1.call-update) | async-done | bytes 524304 | tf_op jit(solution)/shard_map/reduce_scatter | solution.py:214
  1713.0 184.0 %reduce-scatter.11.cloned.1.call-done = f32[128,1024]{1,0:T(8,128)} async-done(((f32[2048,1024]{1,0:T(8,128)}), f32[128,1024]{1,0:T(8,128)}) %reduce-scatter.11.cloned.1.call-update) | async-done | bytes 524304 | tf_op jit(solution)/shard_map/reduce_scatter | solution.py:215
  1897.1 183.1 %reduce-scatter.13.cloned.1.call-done = f32[128,1024]{1,0:T(8,128)} async-done(((f32[2048,1024]{1,0:T(8,128)}), f32[128,1024]{1,0:T(8,128)}) %reduce-scatter.13.cloned.1.call-update) | async-done | bytes 524304 | tf_op jit(solution)/shard_map/reduce_scatter | solution.py:216
  2080.2 183.1 %reduce-scatter.17.cloned.1.call-done = f32[128,1024]{1,0:T(8,128)} async-done(((f32[2048,1024]{1,0:T(8,128)}), f32[128,1024]{1,0:T(8,128)}) %reduce-scatter.17.cloned.1.call-update) | async-done | bytes 524304 | tf_op jit(solution)/shard_map/reduce_scatter | solution.py:218
  2263.3 482.0 %reduce-scatter.19.cloned.1.call-done = f32[128,2816]{1,0:T(8,128)} async-done(((f32[2048,2816]{1,0:T(8,128)}), f32[128,2816]{1,0:T(8,128)}) %reduce-scatter.19.cloned.1.call-update) | async-done | bytes 1441808 | tf_op jit(solution)/shard_map/reduce_scatter | solution.py:219
  2745.2 482.7 %reduce-scatter.21.cloned.1.call-done = f32[128,2816]{1,0:T(8,128)} async-done(((f32[2048,2816]{1,0:T(8,128)}), f32[128,2816]{1,0:T(8,128)}) %reduce-scatter.21.cloned.1.call-update) | async-done | bytes 1441808 | tf_op jit(solution)/shard_map/reduce_scatter | solution.py:220
  3227.9 482.7 %reduce-scatter.23.cloned.1.call-done = f32[128,2816]{1,0:T(8,128)} async-done(((f32[2048,2816]{1,0:T(8,128)}), f32[128,2816]{1,0:T(8,128)}) %reduce-scatter.23.cloned.1.call-update) | async-done | bytes 1441808 | tf_op jit(solution)/shard_map/reduce_scatter | solution.py:221
  (657 shorter events, 338.9 us)
Async XLA Ops:
  7.2 42.6 %copy-start.56 = (bf16[128]{0:T(256)(128)(2,1)S(1)}, bf16[128]{0:T(256)(128)(2,1)}, u32[]{:S(2)}) copy-start(bf16[128]{0:T(256)(128)(2,1)} %param.21) | copy-start | bytes 772
  7.2 83.1 %copy-start.5 = (bf16[512,2048]{1,0:T(8,128)(2,1)S(1)}, bf16[512,2048]{1,0:T(8,128)(2,1)}, u32[]{:S(2)}) copy-start(bf16[512,2048]{1,0:T(8,128)(2,1)} %param.18) | copy-start | bytes 6291460
  7.2 89.1 %all-gather.10.cloned.1.call-start = ((), (), s32[]{:S(2)}) async-start(), calls=%async_computation.8 | async-start | bytes 4456448 | tf_op jit(solution)/shard_map/all_gather | solution.py:128
  7.9 160.5 %all-gather.12.cloned.1.call-start = ((), (), s32[]{:S(2)}) async-start(), calls=%async_computation.9 | async-start | bytes 4456448 | tf_op jit(solution)/shard_map/all_gather | solution.py:129
  8.7 237.2 %all-gather.14.cloned.1.call-start = ((), (), s32[]{:S(2)}) async-start(), calls=%async_computation.10 | async-start | bytes 4456448 | tf_op jit(solution)/shard_map/all_gather | solution.py:127
  9.4 429.2 %all-gather.16.cloned.1.call-start = ((), (), s32[]{:S(2)}) async-start(), calls=%async_computation.11 | async-start | bytes 4456448 | tf_op jit(solution)/shard_map/all_gather | solution.py:131
  10.0 468.0 %all-reduce.9.cloned.1.call-start = ((), (), s32[]{:S(2)}) async-start(), calls=%async_computation.12 | async-start | bytes 8388608 | tf_op jit(solution)/shard_map/psum | solution.py:155
  49.8 41.0 %copy-start.36 = (bf16[2048,128]{1,0:T(8,128)(2,1)}, bf16[2048,128]{1,0:T(8,128)(2,1)S(1)}, u32[]{:S(2)}) copy-start(bf16[2048,128]{1,0:T(8,128)(2,1)S(1)} %all_gather.39) | copy-start | bytes 1572868
  90.3 155.6 %copy-start.46 = (f32[16,1,128]{2,1,0:T(1,128)}, f32[16,1,128]{2,1,0:T(1,128)S(1)}, u32[]{:S(2)}) copy-start(f32[16,1,128]{2,1,0:T(1,128)S(1)} %convert_element_type.104) | copy-start | bytes 24580
  90.8 155.1 %copy-start.50 = (f32[512]{0:T(512)}, f32[512]{0:T(512)S(1)}, u32[]{:S(2)}) copy-start(f32[512]{0:T(512)S(1)} %fusion.151) | copy-start | bytes 6148
  284.2 17.3 copy-start.13
  284.2 17.4 copy-start.25
  328.0 17.3 copy-start.13
  328.0 17.3 copy-start.25
  371.8 17.3 copy-start.13
  371.8 17.4 copy-start.25
  415.6 17.3 copy-start.13
  415.6 17.3 copy-start.25
  445.6 32.3 copy-start.58
  445.6 171.6 %all-gather.18.cloned.1.call-start = ((), (), s32[]{:S(2)}) async-start(), calls=%async_computation.13 | async-start | bytes 12255232 | tf_op jit(solution)/shard_map/all_gather | solution.py:132
  446.2 314.5 %all-gather.20.cloned.1.call-start = ((), (), s32[]{:S(2)}) async-start(), calls=%async_computation.14 | async-start | bytes 12255232 | tf_op jit(solution)/shard_map/all_gather | solution.py:133
  446.9 457.3 %all-gather.22.cloned.1.call-start = ((), (), s32[]{:S(2)}) async-start(), calls=%async_computation.15 | async-start | bytes 12255232 | tf_op jit(solution)/shard_map/all_gather | solution.py:134
  447.7 523.6 %all-reduce.11.cloned.1.call-start = ((), (), s32[]{:S(2)}) async-start(), calls=%async_computation.16 | async-start | bytes 8388608 | tf_op jit(solution)/shard_map/psum | solution.py:187
  478.0 498.5 %copy-start.52 = (f32[512]{0:T(512)}, f32[512]{0:T(512)S(1)}, u32[]{:S(2)}) copy-start(f32[512]{0:T(512)S(1)} %and_convert_fusion) | copy-start | bytes 6148
  483.3 277.4 %copy-start.35 = (bf16[512,2048]{1,0:T(8,128)(2,1)}, bf16[512,2048]{1,0:T(8,128)(2,1)S(1)}, u32[]{:S(2)}) copy-start(bf16[512,2048]{1,0:T(8,128)(2,1)S(1)} %multiply_convert_fusion.3) | copy-start | bytes 6291460
  904.2 28.7 slice-start
  904.2 28.7 slice-start.1
  920.5 12.4 copy-start.65
  920.5 12.4 copy-start.64
  920.5 12.4 slice-start.2
  942.2 546.3 %all-reduce.13.cloned.1.call-start = ((), (), s32[]{:S(2)}) async-start(), calls=%async_computation.25 | async-start | bytes 16777216 | tf_op jit(solution)/shard_map/psum | solution.py:163
  1004.4 12.6 copy-start.28
  1019.3 15.2 copy-start.10
  1043.2 16.9 copy-start.9
  1063.1 15.0 copy-start.17
  1063.1 15.7 copy-start.29
  1063.1 15.7 copy-start.31
  1099.6 12.6 copy-start.28
  1114.5 15.5 copy-start.10
  1138.6 16.8 copy-start.9
  1158.2 15.2 copy-start.17
  1158.2 15.9 copy-start.29
  1158.2 15.9 copy-start.31
  1194.9 12.6 copy-start.28
  1209.8 15.3 copy-start.10
  1233.9 16.9 copy-start.9
  1253.5 15.0 copy-start.17
  1253.6 15.7 copy-start.29
  1253.6 15.7 copy-start.31
  1290.3 12.6 copy-start.28
  1305.2 15.2 copy-start.10
  1329.1 16.9 copy-start.9
  1348.9 15.0 copy-start.17
  1348.9 15.7 copy-start.29
  1349.0 15.7 copy-start.31
  1410.5 163.5 %reduce-scatter.15.cloned.1.call-start = ((), (), s32[]{:S(2)}) async-start(), calls=%async_computation.20 | async-start | bytes 1114112 | tf_op jit(solution)/shard_map/reduce_scatter | solution.py:217
  1414.1 298.9 %reduce-scatter.9.cloned.1.call-start = ((), (), s32[]{:S(2)}) async-start(), calls=%async_computation.17 | async-start | bytes 8912896 | tf_op jit(solution)/shard_map/reduce_scatter | solution.py:214
  1422.0 475.1 %reduce-scatter.11.cloned.1.call-start = ((), (), s32[]{:S(2)}) async-start(), calls=%async_computation.18 | async-start | bytes 8912896 | tf_op jit(solution)/shard_map/reduce_scatter | solution.py:215
  1428.2 651.9 %reduce-scatter.13.cloned.1.call-start = ((), (), s32[]{:S(2)}) async-start(), calls=%async_computation.19 | async-start | bytes 8912896 | tf_op jit(solution)/shard_map/reduce_scatter | solution.py:216
  1435.3 827.9 %reduce-scatter.17.cloned.1.call-start = ((), (), s32[]{:S(2)}) async-start(), calls=%async_computation.21 | async-start | bytes 8912896 | tf_op jit(solution)/shard_map/reduce_scatter | solution.py:218
  1445.6 1299.6 %reduce-scatter.19.cloned.1.call-start = ((), (), s32[]{:S(2)}) async-start(), calls=%async_computation.22 | async-start | bytes 24510464 | tf_op jit(solution)/shard_map/reduce_scatter | solution.py:219
  1459.3 1768.5 %reduce-scatter.21.cloned.1.call-start = ((), (), s32[]{:S(2)}) async-start(), calls=%async_computation.23 | async-start | bytes 24510464 | tf_op jit(solution)/shard_map/reduce_scatter | solution.py:220
  1472.5 2238.1 %reduce-scatter.23.cloned.1.call-start = ((), (), s32[]{:S(2)}) async-start(), calls=%async_computation.24 | async-start | bytes 24510464 | tf_op jit(solution)/shard_map/reduce_scatter | solution.py:221
  1486.6 78.0 %copy-start.55 = (f32[512]{0:T(512)S(1)}, f32[512]{0:T(512)}, u32[]{:S(2)}) copy-start(f32[512]{0:T(512)} %copy-done.54) | copy-start | bytes 6148
  (101 other events, 522.4 us)
Sparse Core Ops, SparseCore 0:
  10.8 80.0 all-gather.9
  93.6 74.7 all-gather.11
  171.2 74.6 all-gather.13
  248.5 74.6 all-gather.15
  445.7 27.3 all-reduce.8
  476.1 141.0 all-gather.17
  620.3 140.3 all-gather.19
  763.8 140.3 all-gather.21
  942.3 28.9 all-reduce.10
  1410.7 40.1 all-reduce.12
  1453.7 67.9 reduce-scatter.14
  1524.5 188.5 reduce-scatter.8
  1716.0 181.0 reduce-scatter.10
  1899.9 180.2 reduce-scatter.12
  2083.0 180.2 reduce-scatter.16
  2266.1 479.0 reduce-scatter.18
  2748.1 479.7 reduce-scatter.20
  3230.7 479.7 reduce-scatter.22
where the time goes:
time: 3730 us; the launch traced here: 3720 us
  waiting for transfers between devices  2680 us (72%)
  matrix products  590 us (16%)
  blocking collectives  177 us (5%)
  local copies, waits for them, and re-layouts  127 us (3%)
  other arithmetic  114 us (3%)
    reduce_scatter x1, waiting for transfers between devices, body(): lax.psum_scatter(grad_down, 'dp', scatter_dimension=0, tiled=True)  483 us
    reduce_scatter x1, waiting for transfers between devices, body(): lax.psum_scatter(grad_up, 'dp', scatter_dimension=0, tiled=True)  483 us
    reduce_scatter x1, waiting for transfers between devices, body(): lax.psum_scatter(grad_gate, 'dp', scatter_dimension=0, tiled=True)  482 us
    dot_general x104, matrix products, einsum_high(): return jnp.einsum(form, left, right, precision=lax.Precision.HIGHEST)  406 us
    reduce_scatter x1, waiting for transfers between devices, body(): lax.psum_scatter(grad_key, 'dp', scatter_dimension=0, tiled=True)  184 us
    reduce_scatter x1, waiting for transfers between devices, body(): lax.psum_scatter(grad_value, 'dp', scatter_dimension=0, tiled=True)  183 us
    reduce_scatter x1, waiting for transfers between devices, body(): lax.psum_scatter(grad_out, 'dp', scatter_dimension=0, tiled=True)  183 us
    reduce_scatter x1, waiting for transfers between devices, body(): lax.psum_scatter(grad_query, 'dp', scatter_dimension=0, tiled=True)  139 us
  transfers between devices with their start and end apart: 18, of which 13 were waited for; matrix products, arithmetic and copies ran while one was open for 9% of the time, Pallas kernels for 0%

commit v1 on v0

--- a/solution.py
+++ b/solution.py
@@ -6,6 +6,18 @@
 SLOTS = 64
 KDIM = 512
 SEQ_LEN = 256
+
+
+def collect(value, axis, dim):
+    ways, here = (lax.axis_size(axis), lax.axis_index(axis))
+    grown, reach = (value, 1)
+    while reach < ways:
+        theirs = lax.ppermute(grown, axis, [(d, d ^ reach) for d in range(ways)])
+        mine_first = jnp.concatenate([grown, theirs], axis=dim)
+        theirs_first = jnp.concatenate([theirs, grown], axis=dim)
+        grown = jnp.where(here & reach == 0, mine_first, theirs_first)
+        reach = 2 * reach
+    return grown
 
 
 def einsum_high(form, left, right):
@@ -129,7 +141,7 @@
         lax.all_gather(shards[4], "dp", axis=0, tiled=True),
         lax.all_gather(shards[5], "dp", axis=0, tiled=True),
         lax.all_gather(shards[6], "dp", axis=0, tiled=True),
-        lax.all_gather(shards[7], "dp", axis=0, tiled=True),
+        collect(shards[7], "dp", 0),
         lax.all_gather(shards[8], "dp", axis=0, tiled=True),
         lax.all_gather(shards[9], "dp", axis=0, tiled=True),
     )

time: 3730 us -> 3940 us (1.056)
  blocking collectives: 177 us -> 531 us
  waiting for transfers between devices: 2680 us -> 2510 us
    all_gather x1, blocking collectives: 29.5 us -> 384 us  [body(): lax.all_gather(shards[1], 'dp', axis=0, tiled=True)]
    ppermute x0 -> x4, waiting for transfers between devices: none -> 190 us  [collect(): theirs = lax.ppermute(grown, axis, [(d, d ^ reach) for d in range(ways)])]
    all_gather x1, waiting for transfers between devices: 132 us -> 0.01 us  [body(): lax.all_gather(shards[9], 'dp', axis=0, tiled=True)]
    all_gather x1, waiting for transfers between devices: 132 us -> 0.02 us  [body(): lax.all_gather(shards[8], 'dp', axis=0, tiled=True)]
    all_gather x1, waiting for transfers between devices: 134 us -> 40.8 us  [body(): lax.all_gather(shards[7], 'dp', axis=0, tiled=True)]
  transfers between devices with their start and end apart: 18 -> 22, of which waited for: 13 -> 14; matrix products, arithmetic and copies ran while one was open for 9% -> 10% of each run, Pallas kernels for 0% -> 0%
where the time goes in v1:
time: 3940 us; the launch traced here: 3930 us
  waiting for transfers between devices  2510 us (64%)
  matrix products  594 us (15%)
  blocking collectives  531 us (13%)
  other arithmetic  129 us (3%)
  local copies, waits for them, and re-layouts  127 us (3%)
    reduce_scatter x1, waiting for transfers between devices, body(): lax.psum_scatter(grad_down, 'dp', scatter_dimension=0, tiled=True)  483 us
    reduce_scatter x1, waiting for transfers between devices, body(): lax.psum_scatter(grad_up, 'dp', scatter_dimension=0, tiled=True)  483 us
    reduce_scatter x1, waiting for transfers between devices, body(): lax.psum_scatter(grad_gate, 'dp', scatter_dimension=0, tiled=True)  482 us
    dot_general x104, matrix products, einsum_high(): return jnp.einsum(form, left, right, precision=lax.Precision.HIGHEST)  406 us
    all_gather x1, blocking collectives, body(): lax.all_gather(shards[1], 'dp', axis=0, tiled=True)  384 us
    ppermute x4, waiting for transfers between devices, collect(): theirs = lax.ppermute(grown, axis, [(d, d ^ reach) for d in range(ways)])  190 us
    reduce_scatter x1, waiting for transfers between devices, body(): lax.psum_scatter(grad_key, 'dp', scatter_dimension=0, tiled=True)  184 us
    reduce_scatter x1, waiting for transfers between devices, body(): lax.psum_scatter(grad_value, 'dp', scatter_dimension=0, tiled=True)  183 us
  transfers between devices with their start and end apart: 22, of which 14 were waited for; matrix products, arithmetic and copies ran while one was open for 10% of the time, Pallas kernels for 0%

profile of v1, /device:TPU:10, one launch (start us, length us, event | category | flops | bytes accessed | tf_op | source)
XLA Modules:
  0.0 3934.6 jit_solution(2170725380270090385)
XLA Ops:
  14.0 35.8 all_gather.38
  49.8 40.5 %all-gather = bf16[16,1,128]{2,1,0:T(2,128)(2,1)S(1)} all-gather(bf16[1,1,128]{2,1,0:T(2,128)(2,1)S(1)} %bitcast.436), channel_id=1, replica_groups=mesh['dp'=16,'head'=2] {'dp'}, dimensions={0}, use_global_device_ids=true | all-gather | bytes 4352 | tf_op jit(solution)/shard_map/all_gather | solution.py:137
  96.4 6.8 fusion.139
  110.8 57.6 %all-gather.12.cloned.1.call-done = bf16[2048,1024]{1,0:T(8,128)(2,1)} async-done(((bf16[128,1024]{1,0:T(8,128)(2,1)}), bf16[2048,1024]{1,0:T(8,128)(2,1)}) %all-gather.12.cloned.1.call-update) | async-done | bytes 4194320 | tf_op jit(solution)/shard_map/all_gather | solution.py:141
  181.9 64.0 %all-gather.14.cloned.1.call-done = bf16[2048,1024]{1,0:T(8,128)(2,1)} async-done(((bf16[128,1024]{1,0:T(8,128)(2,1)}), bf16[2048,1024]{1,0:T(8,128)(2,1)}) %all-gather.14.cloned.1.call-update) | async-done | bytes 4194320 | tf_op jit(solution)/shard_map/all_gather | solution.py:139
  245.9 6.8 multiply_multiply_fusion.1
  260.2 175.8 %while.48 = (s32[]{:T(128)}, f32[4,64,512]{2,1,0:T(8,128)S(1)}, f32[4,64,512]{2,1,0:T(8,128)S(1)}, bf16[4,4,64,512]{3,2,0,1:T(8,128)(2,1)}, f32[4,4,64,512]{3,2,...) while((s32[]{:T(128)}, f32[4,64,512]{2,1,0:T(8,128)S(1)}, ...), condition=%wide.region_6.7_spmd.clone.clone, body=%wide.region_2.6_spmd.clone.clone.sunk | while | flops 640237632 | bytes 21779780 | solution.py:86
  265.7 10.1 fusion.408
  284.2 15.7 fusion.412
  309.5 10.1 fusion.408
  328.0 15.7 fusion.412
  353.3 10.1 fusion.408
  371.8 15.7 fusion.412
  397.1 10.1 fusion.408
  415.6 15.7 fusion.412
  438.6 6.9 fusion.188
  448.3 16.3 collective-permute-done
  467.7 35.7 collective-permute-done.1
  507.3 137.8 %collective-permute-done.2 = bf16[512,2816]{1,0:T(8,128)(2,1)} collective-permute-done((bf16[512,2816]{1,0:T(8,128)(2,1)}, bf16[512,2816]{1,0:T(8,128)(2,1)}, u32[]{:S(2)}, u32[]{:S(2)}) %collective-permute-start.2) | collective-permute-done | bytes 2883616 | tf_op jit(solution)/shard_map/ppermute | solution.py:15
  645.0 9.1 maximum_select_fusion.2
  654.1 11.0 collective-permute-start.3
  665.8 383.6 %all-gather.1 = bf16[16,1,128]{2,1,0:T(2,128)(2,1)S(1)} all-gather(bf16[1,1,128]{2,1,0:T(2,128)(2,1)S(1)} %bitcast.437), channel_id=1, replica_groups=mesh['dp'=16,'head'=2] {'dp'}, dimensions={0}, use_global_device_ids=true | all-gather | bytes 4352 | tf_op jit(solution)/shard_map/all_gather | solution.py:138
  1054.9 11.9 fusion.189
  1066.8 12.9 fusion.162
  1079.7 18.9 multiply_convert_fusion
  1098.5 40.8 %all-gather.22.cloned.1.call-done = bf16[2048,2816]{1,0:T(8,128)(2,1)} async-done(((bf16[128,2816]{1,0:T(8,128)(2,1)}), bf16[2048,2816]{1,0:T(8,128)(2,1)}) %all-gather.22.cloned.1.call-update) | async-done | bytes 11534352 | tf_op jit(solution)/shard_map/all_gather | solution.py:185
  1139.4 10.0 fusion.191
  1149.4 10.4 convolution_add_fusion.8
  1159.9 11.6 fusion.190
  1171.5 17.4 all-reduce.11.cloned.1.call-done
  1212.9 388.9 %while.47 = (s32[]{:T(128)}, f32[4,64,512]{2,1,0:T(8,128)S(1)}, f32[4,64,512]{2,1,0:T(8,128)}, f32[4,4,64,512]{3,2,0,1:T(8,128)}, f32[4,4,64,512]{3,2,0,1:T(8,12...) while((s32[]{:T(128)}, f32[4,64,512]{2,1,0:T(8,128)S(1)}, ...), condition=%wide.region_24.25_spmd.clone, body=%wide.region_12.24_spmd.clone.sunk | while | flops 1495470592 | bytes 52910904 | solution.py:86
  1225.3 9.1 fusion.379
  1241.8 10.1 fusion.383
  1260.8 15.4 fusion.386
  1280.5 14.9 fusion.391
  1296.2 6.4 fusion.393
  1320.7 9.1 fusion.379
  1337.2 10.1 fusion.383
  1356.0 15.4 fusion.386
  1375.9 14.9 fusion.391
  1391.6 6.4 fusion.393
  1415.9 9.1 fusion.379
  1432.6 10.1 fusion.383
  1451.4 15.4 fusion.386
  1471.1 15.1 fusion.391
  1487.0 6.4 fusion.393
  1511.2 9.1 fusion.379
  1527.8 10.1 fusion.383
  1546.8 15.4 fusion.386
  1566.4 14.9 fusion.391
  1631.7 7.8 fusion.169
  1654.1 9.0 fusion.140
  1663.2 13.6 fusion.195
  1676.9 13.1 fusion.196
  1690.7 13.4 fusion.161
  1709.5 71.6 %all-reduce.3 = (f32[2048]{0:T(1024)S(1)}, f32[2048]{0:T(1024)S(1)}) all-reduce(f32[2048]{0:T(1024)S(1)} %get-tuple-element.678, f32[2048]{0:T(1024)S(1)} %copy-done.50), channel_id=2, replica_groups=mesh['dp'=16,'head'=2] {'dp'}, use_global_device_ids=true, to_apply=%region_28.29.clone | all-reduce | flops 4096 | bytes 32768
  1782.3 9.5 fusion.130
  1791.8 138.4 %reduce-scatter.9.cloned.1.call-done = f32[128,1024]{1,0:T(8,128)} async-done(((f32[2048,1024]{1,0:T(8,128)}), f32[128,1024]{1,0:T(8,128)}) %reduce-scatter.9.cloned.1.call-update) | async-done | bytes 524304 | tf_op jit(solution)/shard_map/reduce_scatter | solution.py:226
  1930.2 184.0 %reduce-scatter.11.cloned.1.call-done = f32[128,1024]{1,0:T(8,128)} async-done(((f32[2048,1024]{1,0:T(8,128)}), f32[128,1024]{1,0:T(8,128)}) %reduce-scatter.11.cloned.1.call-update) | async-done | bytes 524304 | tf_op jit(solution)/shard_map/reduce_scatter | solution.py:227
  2114.2 183.1 %reduce-scatter.13.cloned.1.call-done = f32[128,1024]{1,0:T(8,128)} async-done(((f32[2048,1024]{1,0:T(8,128)}), f32[128,1024]{1,0:T(8,128)}) %reduce-scatter.13.cloned.1.call-update) | async-done | bytes 524304 | tf_op jit(solution)/shard_map/reduce_scatter | solution.py:228
  2297.3 183.1 %reduce-scatter.17.cloned.1.call-done = f32[128,1024]{1,0:T(8,128)} async-done(((f32[2048,1024]{1,0:T(8,128)}), f32[128,1024]{1,0:T(8,128)}) %reduce-scatter.17.cloned.1.call-update) | async-done | bytes 524304 | tf_op jit(solution)/shard_map/reduce_scatter | solution.py:230
  2480.4 482.0 %reduce-scatter.19.cloned.1.call-done = f32[128,2816]{1,0:T(8,128)} async-done(((f32[2048,2816]{1,0:T(8,128)}), f32[128,2816]{1,0:T(8,128)}) %reduce-scatter.19.cloned.1.call-update) | async-done | bytes 1441808 | tf_op jit(solution)/shard_map/reduce_scatter | solution.py:231
  2962.3 482.6 %reduce-scatter.21.cloned.1.call-done = f32[128,2816]{1,0:T(8,128)} async-done(((f32[2048,2816]{1,0:T(8,128)}), f32[128,2816]{1,0:T(8,128)}) %reduce-scatter.21.cloned.1.call-update) | async-done | bytes 1441808 | tf_op jit(solution)/shard_map/reduce_scatter | solution.py:232
  3445.0 482.6 %reduce-scatter.23.cloned.1.call-done = f32[128,2816]{1,0:T(8,128)} async-done(((f32[2048,2816]{1,0:T(8,128)}), f32[128,2816]{1,0:T(8,128)}) %reduce-scatter.23.cloned.1.call-update) | async-done | bytes 1441808 | tf_op jit(solution)/shard_map/reduce_scatter | solution.py:233
  (661 shorter events, 365.1 us)
Async XLA Ops:
  7.2 42.6 %copy-start.57 = (bf16[128]{0:T(256)(128)(2,1)S(1)}, bf16[128]{0:T(256)(128)(2,1)}, u32[]{:S(2)}) copy-start(bf16[128]{0:T(256)(128)(2,1)} %param.21) | copy-start | bytes 772
  7.2 83.1 %copy-start.5 = (bf16[512,2048]{1,0:T(8,128)(2,1)S(1)}, bf16[512,2048]{1,0:T(8,128)(2,1)}, u32[]{:S(2)}) copy-start(bf16[512,2048]{1,0:T(8,128)(2,1)} %param.18) | copy-start | bytes 6291460
  7.2 89.1 %all-gather.10.cloned.1.call-start = ((), (), s32[]{:S(2)}) async-start(), calls=%async_computation.8 | async-start | bytes 4456448 | tf_op jit(solution)/shard_map/all_gather | solution.py:140
  7.9 160.5 %all-gather.12.cloned.1.call-start = ((), (), s32[]{:S(2)}) async-start(), calls=%async_computation.9 | async-start | bytes 4456448 | tf_op jit(solution)/shard_map/all_gather | solution.py:141
  8.7 237.2 %all-gather.14.cloned.1.call-start = ((), (), s32[]{:S(2)}) async-start(), calls=%async_computation.10 | async-start | bytes 4456448 | tf_op jit(solution)/shard_map/all_gather | solution.py:139
  9.4 429.2 %all-gather.16.cloned.1.call-start = ((), (), s32[]{:S(2)}) async-start(), calls=%async_computation.11 | async-start | bytes 4456448 | tf_op jit(solution)/shard_map/all_gather | solution.py:143
  10.0 1039.6 %all-reduce.9.cloned.1.call-start = ((), (), s32[]{:S(2)}) async-start(), calls=%async_computation.12 | async-start | bytes 8388608 | tf_op jit(solution)/shard_map/psum | solution.py:167
  49.8 41.0 %copy-start.37 = (bf16[2048,128]{1,0:T(8,128)(2,1)}, bf16[2048,128]{1,0:T(8,128)(2,1)S(1)}, u32[]{:S(2)}) copy-start(bf16[2048,128]{1,0:T(8,128)(2,1)S(1)} %all_gather.38) | copy-start | bytes 1572868
  90.3 155.6 %copy-start.47 = (f32[16,1,128]{2,1,0:T(1,128)}, f32[16,1,128]{2,1,0:T(1,128)S(1)}, u32[]{:S(2)}) copy-start(f32[16,1,128]{2,1,0:T(1,128)S(1)} %convert_element_type.104) | copy-start | bytes 24580
  90.8 155.1 %copy-start.51 = (f32[512]{0:T(512)}, f32[512]{0:T(512)S(1)}, u32[]{:S(2)}) copy-start(f32[512]{0:T(512)S(1)} %fusion.158) | copy-start | bytes 6148
  284.2 17.3 copy-start.13
  284.2 17.4 copy-start.25
  328.0 17.3 copy-start.13
  328.0 17.4 copy-start.25
  371.8 17.3 copy-start.13
  371.8 17.3 copy-start.25
  415.6 17.3 copy-start.13
  415.6 17.3 copy-start.25
  445.6 609.3 %all-gather.18.cloned.1.call-start = ((), (), s32[]{:S(2)}) async-start(), calls=%async_computation.13 | async-start | bytes 12255232 | tf_op jit(solution)/shard_map/all_gather | solution.py:145
  446.1 620.6 %all-gather.20.cloned.1.call-start = ((), (), s32[]{:S(2)}) async-start(), calls=%async_computation.14 | async-start | bytes 12255232 | tf_op jit(solution)/shard_map/all_gather | solution.py:146
  446.9 692.5 %all-gather.22.cloned.1.call-start = ((), (), s32[]{:S(2)}) async-start(), calls=%async_computation.15 | async-start | bytes 12255232 | tf_op jit(solution)/shard_map/all_gather | solution.py:185
  447.6 741.3 %all-reduce.11.cloned.1.call-start = ((), (), s32[]{:S(2)}) async-start(), calls=%async_computation.16 | async-start | bytes 8388608 | tf_op jit(solution)/shard_map/psum | solution.py:199
  447.7 17.0 collective-permute-start
  467.1 36.4 collective-permute-start.1
  506.8 138.2 %collective-permute-start.2 = (bf16[512,2816]{1,0:T(8,128)(2,1)}, bf16[512,2816]{1,0:T(8,128)(2,1)}, u32[]{:S(2)}, u32[]{:S(2)}) collective-permute-start(bf16[512,2816]{1,0:T(8,128)(2,1)} %maximum_select_fusion.3), channel_id=1, source_target_pairs={{0,8},{2,10},{4,12},{6,14},{8,0},{10,2},{12,4},{14,6},{16,24},{18,... | collective-permute-start | bytes 8650760 | tf_op jit(solution)/shard_map/ppermute | solution.py:15
  507.3 158.5 %copy-start.58 = (bf16[128]{0:T(256)(128)(2,1)S(1)}, bf16[128]{0:T(256)(128)(2,1)}, u32[]{:S(2)}) copy-start(bf16[128]{0:T(256)(128)(2,1)} %param.22) | copy-start | bytes 772
  507.3 542.2 %copy-start.59 = (s32[2]{0:T(128)S(1)}, s32[2]{0:T(128)}, u32[]{:S(2)}) copy-start(s32[2]{0:T(128)} %param.20) | copy-start | bytes 28
  654.1 425.5 %collective-permute-start.3 = (bf16[1024,2816]{1,0:T(8,128)(2,1)}, bf16[1024,2816]{1,0:T(8,128)(2,1)}, u32[]{:S(2)}, u32[]{:S(2)}) collective-permute-start(bf16[1024,2816]{1,0:T(8,128)(2,1)} %maximum_select_fusion.2), channel_id=1, source_target_pairs={{0,16},{2,18},{4,20},{6,22},{8,24},{10,26},{12,28},{14,30},{16,0},... | collective-permute-start | bytes 17301512 | tf_op jit(solution)/shard_map/ppermute | solution.py:15
  1049.5 144.6 %copy-start.53 = (f32[512]{0:T(512)}, f32[512]{0:T(512)S(1)}, u32[]{:S(2)}) copy-start(f32[512]{0:T(512)S(1)} %and_convert_fusion) | copy-start | bytes 6148
  1054.9 24.8 copy-start.36
  1159.8 546.2 %all-reduce.13.cloned.1.call-start = ((), (), s32[]{:S(2)}) async-start(), calls=%async_computation.25 | async-start | bytes 16777216 | tf_op jit(solution)/shard_map/psum | solution.py:175
  1221.8 12.6 copy-start.28
  1236.7 15.3 copy-start.10
  1260.8 16.9 copy-start.9
  1280.5 15.0 copy-start.17
  1280.5 15.7 copy-start.29
  1280.5 15.7 copy-start.31
  1317.2 12.6 copy-start.28
  1332.1 15.2 copy-start.10
  1356.0 16.8 copy-start.9
  1375.9 15.0 copy-start.17
  1375.9 15.7 copy-start.29
  1375.9 15.7 copy-start.31
  1412.4 12.6 copy-start.28
  1427.3 15.4 copy-start.10
  1451.4 16.9 copy-start.9
  1471.0 15.2 copy-start.17
  1471.1 15.9 copy-start.29
  1471.1 15.9 copy-start.31
  1507.8 12.6 copy-start.28
  1522.7 15.3 copy-start.10
  1546.8 16.8 copy-start.9
  1566.4 15.0 copy-start.17
  1566.4 15.7 copy-start.29
  1566.4 15.7 copy-start.31
  1628.0 163.8 %reduce-scatter.15.cloned.1.call-start = ((), (), s32[]{:S(2)}) async-start(), calls=%async_computation.20 | async-start | bytes 1114112 | tf_op jit(solution)/shard_map/reduce_scatter | solution.py:229
  1631.6 298.5 %reduce-scatter.9.cloned.1.call-start = ((), (), s32[]{:S(2)}) async-start(), calls=%async_computation.17 | async-start | bytes 8912896 | tf_op jit(solution)/shard_map/reduce_scatter | solution.py:226
  1639.5 474.7 %reduce-scatter.11.cloned.1.call-start = ((), (), s32[]{:S(2)}) async-start(), calls=%async_computation.18 | async-start | bytes 8912896 | tf_op jit(solution)/shard_map/reduce_scatter | solution.py:227
  1645.7 651.5 %reduce-scatter.13.cloned.1.call-start = ((), (), s32[]{:S(2)}) async-start(), calls=%async_computation.19 | async-start | bytes 8912896 | tf_op jit(solution)/shard_map/reduce_scatter | solution.py:228
  1652.8 827.6 %reduce-scatter.17.cloned.1.call-start = ((), (), s32[]{:S(2)}) async-start(), calls=%async_computation.21 | async-start | bytes 8912896 | tf_op jit(solution)/shard_map/reduce_scatter | solution.py:230
  1663.1 1299.2 %reduce-scatter.19.cloned.1.call-start = ((), (), s32[]{:S(2)}) async-start(), calls=%async_computation.22 | async-start | bytes 24510464 | tf_op jit(solution)/shard_map/reduce_scatter | solution.py:231
  1676.8 1768.1 %reduce-scatter.21.cloned.1.call-start = ((), (), s32[]{:S(2)}) async-start(), calls=%async_computation.23 | async-start | bytes 24510464 | tf_op jit(solution)/shard_map/reduce_scatter | solution.py:232
  1690.0 2237.6 %reduce-scatter.23.cloned.1.call-start = ((), (), s32[]{:S(2)}) async-start(), calls=%async_computation.24 | async-start | bytes 24510464 | tf_op jit(solution)/shard_map/reduce_scatter | solution.py:233
  1704.1 78.2 %copy-start.56 = (f32[512]{0:T(512)S(1)}, f32[512]{0:T(512)}, u32[]{:S(2)}) copy-start(f32[512]{0:T(512)} %copy-done.55) | copy-start | bytes 6148
  (102 other events, 532.1 us)
Sparse Core Ops, SparseCore 0:
  10.8 80.0 all-gather.9
  93.6 74.7 all-gather.11
  171.2 74.6 all-gather.13
  248.5 74.6 all-gather.15
  445.7 27.4 all-reduce.8
  476.1 193.7 all-gather.17
  673.0 290.2 all-gather.19
  966.5 172.8 all-gather.21
  1159.9 28.9 all-reduce.10
  1628.2 40.1 all-reduce.12
  1671.2 68.0 reduce-scatter.14
  1742.1 188.0 reduce-scatter.8
  1933.1 181.0 reduce-scatter.10
  2117.0 180.2 reduce-scatter.12
  2300.1 180.2 reduce-scatter.16
  2483.2 479.0 reduce-scatter.18
  2965.2 479.7 reduce-scatter.20
  3447.8 479.7 reduce-scatter.22
